TPU v7x, 32 devices: a whole 2x2x4 slice. The times are simulated.
32 devices in a mesh: groups: 2 (over x), seq: 16 (over z, y, core).
Axes of the slice: x: 2, y: 2, z: 4, core: 2. Of those that a mesh axis runs over, the one named last changes fastest.
Arguments:
- signal: bfloat16 [16384, 2048], P(('groups', 'seq')), parts along dimension 0, may hold values from -6 to 6
- gate_input: bfloat16 [16384, 2048], P(('groups', 'seq')), parts along dimension 0, may hold values from -6 to 6
- cotangent: bfloat16 [16384, 2048], P(('groups', 'seq')), parts along dimension 0, may hold values from -6 to 6
- block_factor: bfloat16 [512, 512], replicated, may hold values from -0.25 to 0.25
- cross_factor: bfloat16 [512, 16, 16], P('seq'), may hold values from -1.5 to 1.5
- order_table: int32 [512], replicated, may hold values from 0 to 511, each once
Outputs:
- grad_signal: bfloat16 [16384, 2048], P(('groups', 'seq')), parts along dimension 0
- grad_gate: bfloat16 [16384, 2048], P(('groups', 'seq')), parts along dimension 0
- grad_block: float32 [1024, 512], P('groups'), parts along dimension 0
- grad_cross: float32 [512, 32, 16], P('seq', 'groups'), parts along dimension 1
There are 2 independent parts, one for each index of `groups`. A program takes and returns all parts, laid end to end along the dimension named above; an argument that names none is the same for every part. Nothing has to cross between parts.
Inputs may be any that keep to these rules, and one draw needn't show every extreme that they name: order_table holds every number of 0 to 511 exactly once.
All inputs are finite; a program needn't handle non-finite values.
Results may differ from a plain program's by a relative error of at most 0.0057.
Values may be sent and summed in bfloat16 or wider, within the bound.
A program may use at most 64 MiB of HBM per device.

v0:
```python
import math
import jax
import jax.numpy as jnp
from jax import lax
from jax.sharding import PartitionSpec as P


def per_device(signal, gate_input, cotangent, block_factor, cross_factor, order_table):
    f32 = jnp.float32
    bf16 = jnp.bfloat16
    count = lax.axis_size("seq")
    width = signal.shape[1]
    permuted = jnp.take(signal, order_table, axis=0)
    mixed = jnp.dot(block_factor, permuted, preferred_element_type=f32).astype(bf16)
    gate_grad = (cotangent.astype(f32) * gate_input.astype(f32)).astype(bf16)
    spread_mixed = lax.all_to_all(mixed[None], "seq", split_axis=1, concat_axis=0, tiled=True)
    spread_grad = lax.all_to_all(gate_grad[None], "seq", split_axis=1, concat_axis=0, tiled=True)
    gated = jnp.einsum(
        "cij,jcd->icd", cross_factor, spread_mixed, preferred_element_type=f32
    ).astype(bf16)
    gated_home = lax.all_to_all(gated, "seq", split_axis=0, concat_axis=1, tiled=True)
    grad_cross = jnp.einsum(
        "icd,jcd->cij", spread_grad, spread_mixed, preferred_element_type=f32
    ) / math.sqrt(width)
    back = jnp.einsum("cij,icd->jcd", cross_factor, spread_grad, preferred_element_type=f32).astype(
        bf16
    )
    back_home = lax.all_to_all(back, "seq", split_axis=0, concat_axis=1, tiled=True)
    grad_gate = (cotangent.astype(f32) * gated_home[0].astype(f32)).astype(bf16)
    back_rows = back_home[0]
    partial_block = lax.dot_general(
        back_rows, permuted, (((1,), (1,)), ((), ())), preferred_element_type=f32
    )
    grad_block = lax.psum(partial_block, "seq") / math.sqrt(count * width)
    spread = lax.dot_general(
        block_factor, back_rows, (((0,), (0,)), ((), ())), preferred_element_type=f32
    ).astype(bf16)
    grad_signal = jnp.zeros_like(spread).at[order_table].set(spread)
    return (grad_signal, grad_gate, grad_block, grad_cross)


def solution(mesh):
    in_specs = (
        P(("groups", "seq"), None),
        P(("groups", "seq"), None),
        P(("groups", "seq"), None),
        P(),
        P("seq", None, None),
        P(),
    )
    out_specs = (
        P(("groups", "seq"), None),
        P(("groups", "seq"), None),
        P("groups", None),
        P("seq", "groups", None),
    )
    return jax.shard_map(
        per_device, mesh=mesh, in_specs=in_specs, out_specs=out_specs, check_vma=False
    )
```

profile of v0, /device:TPU:0, one launch (start us, length us, event | category | flops | bytes accessed | tf_op | source)
XLA Modules:
  0.0 409.7 jit_solution(3647754906035799778)
XLA Ops:
  7.2 0.0 copy-start
  7.2 0.8 compare_and_fusion
  8.0 0.7 compare_select_fusion
  8.7 0.1 copy-done
  8.8 3.3 gather_fusion
  12.1 0.0 copy-done.10
  12.1 3.1 fusion.3
  15.1 7.7 %copy.32 = bf16[1,512,2048]{2,0,1:T(2,128)(2,1)} copy(bf16[1,512,2048]{1,2,0:T(8,128)(2,1)S(1)} %fusion.3) | data formatting | bytes 4194304 | tf_op jit(solution)/shard_map/broadcast_in_dim | solution.py:16
  22.9 0.5 broadcast.9
  23.4 13.2 %reduce = bf16[512,2048]{1,0:T(8,128)(2,1)S(1)} reduce(bf16[512,1,2048]{2,1,0:T(2,128)(2,1)} %bitcast.31, bf16[]{:T(256)} %broadcast.9), dimensions={1}, to_apply=%bitcast.20.reduce_sub_computation | reduce | bytes 4194306
  36.5 2.8 reshape.52
  39.3 7.5 %all-to-all-start.2 = ((bf16[16,2,32768]{2,1,0:T(2,128)(2,1)}), bf16[16,2,32768]{2,1,0:T(2,128)(2,1)S(1)}, u32[]{:S(2)}, u32[]{:S(2)}) async-start(bf16[16,2,32768]{2,1,0:T(2,128)(2,1)} %reshape.52), calls=%async_computation.2 | async-start | bytes 4194304 | tf_op jit(solution)/shard_map/all_to_all | solution.py:16
  46.8 0.0 all-reduce.2.cloned.1.call-start
  46.9 0.0 copy-done.9
  46.9 0.2 copy.34
  47.1 40.9 %all-to-all-done.2 = bf16[16,2,32768]{2,1,0:T(2,128)(2,1)S(1)} async-done(((bf16[16,2,32768]{2,1,0:T(2,128)(2,1)}), bf16[16,2,32768]{2,1,0:T(2,128)(2,1)S(1)}, u32[]{:S(2)}, u32[]{:S(2)}) %all-to-all-start.2) | async-done | bytes 2097184 | tf_op jit(solution)/shard_map/all_to_all | solution.py:16
  87.9 6.7 %reshape.53 = bf16[512,1,2048]{2,1,0:T(2,128)(2,1)} reshape(bf16[16,2,32768]{2,1,0:T(2,128)(2,1)S(1)} %all-to-all-done.2) | data formatting | bytes 4194304
  94.7 3.5 copy.40
  98.1 0.0 copy-start.2
  98.1 2.4 fusion.5
  100.6 0.0 copy-done.2
  100.6 1.2 copy.35
  101.7 0.0 copy-start.5
  101.8 0.0 copy-start.6
  101.8 58.6 %all_to_all.42 = bf16[16,32,2048]{2,1,0:T(8,128)(2,1)S(1)} all-to-all(bf16[16,32,2048]{2,1,0:T(8,128)(2,1)S(1)} %copy.35), channel_id=1, replica_groups=mesh['groups'=2,'seq'=16] {'seq'}, dimensions={0} | all-to-all | bytes 4194304 | tf_op jit(solution)/shard_map/all_to_all | solution.py:21
  160.4 0.0 copy-done.5
  160.4 3.0 fusion.1
  163.3 5.2 %copy.54 = bf16[1,512,2048]{2,0,1:T(2,128)(2,1)} copy(bf16[1,512,2048]{2,1,0:T(8,128)(2,1)S(1)} %get-tuple-element.17) | data formatting | bytes 4194304 | tf_op jit(solution)/shard_map/broadcast_in_dim | solution.py:17
  168.5 13.2 %reduce.1 = bf16[512,2048]{1,0:T(8,128)(2,1)S(1)} reduce(bf16[512,1,2048]{2,1,0:T(2,128)(2,1)} %bitcast.32, bf16[]{:T(256)} %broadcast.9), dimensions={1}, to_apply=%bitcast.29.reduce_sub_computation | reduce | bytes 4194306
  181.7 2.8 reshape.50
  184.4 52.4 %all_to_all.43 = bf16[16,2,32768]{2,1,0:T(2,128)(2,1)S(1)} all-to-all(bf16[16,2,32768]{2,1,0:T(2,128)(2,1)} %reshape.50), channel_id=1, replica_groups=mesh['groups'=2,'seq'=16] {'seq'}, dimensions={0} | all-to-all | bytes 4194304 | tf_op jit(solution)/shard_map/all_to_all | solution.py:17
  236.9 6.7 %reshape.51 = bf16[512,1,2048]{2,1,0:T(2,128)(2,1)} reshape(bf16[16,2,32768]{2,1,0:T(2,128)(2,1)S(1)} %all_to_all.43) | data formatting | bytes 4194304
  243.6 3.5 copy.39
  247.1 2.4 fusion.4
  249.5 0.0 copy-done.4
  249.5 1.2 copy.30
  250.6 0.0 copy-start.7
  250.7 52.4 %all_to_all.44 = bf16[16,32,2048]{2,1,0:T(8,128)(2,1)S(1)} all-to-all(bf16[16,32,2048]{2,1,0:T(8,128)(2,1)S(1)} %copy.30), channel_id=1, replica_groups=mesh['groups'=2,'seq'=16] {'seq'}, dimensions={0} | all-to-all | bytes 4194304 | tf_op jit(solution)/shard_map/all_to_all | solution.py:28
  303.0 1.4 copy-done.8
  304.4 2.3 fusion.19
  306.7 0.0 all-reduce.2.cloned.1.call-update
  306.7 3.9 fusion.12
  310.6 0.8 copy.38
  311.5 4.3 %fusion.2 = bf16[512,2048]{0,1:T(8,128)(2,1)} fusion(bf16[512,2048]{1,0:T(8,128)(2,1)} %bitcast.40, bf16[512,512]{1,0:T(8,128)(2,1)S(1)} %copy-done.10), kind=kOutput, calls=%fused_computation.10 | convolution fusion | flops 1074790400 | bytes 4718592 | tf_op jit(solution)/shard_map/dot_general | solution.py:35
  315.8 4.1 %copy.31 = bf16[512,2048]{1,0:T(8,128)(2,1)} copy(bf16[512,2048]{0,1:T(8,128)(2,1)} %fusion.2) | data formatting | bytes 4194304 | tf_op jit(solution)/shard_map/convert_element_type | solution.py:37
  319.9 6.1 %scatter_custom_fusion = bf16[512,2048]{1,0:T(8,128)(2,1)} fusion(s32[512]{0:T(512)S(1)} %compare_select_fusion, bf16[512,2048]{1,0:T(8,128)(2,1)} %copy.31, bf16[]{:T(256)} %constant.8.clone.1), kind=kCustom, calls=%fused_computation.22 | custom fusion | bytes 2097664 | tf_op jit(solution)/shard_map/scatter | solution.py:38
  326.0 74.5 %all-reduce.2.cloned.1.call-done = f32[512,512]{1,0:T(8,128)} async-done(((f32[512,512]{1,0:T(8,128)}), f32[512,512]{1,0:T(8,128)}) %all-reduce.2.cloned.1.call-update) | async-done | bytes 1048592 | tf_op jit(solution)/shard_map/psum | solution.py:34
  400.6 2.3 broadcast_multiply_fusion
  (11 shorter events, 0.0 us)
Async XLA Ops:
  7.2 1.6 copy-start
  8.8 3.3 copy-start.10
  39.3 7.6 %copy-start.9 = (bf16[32,16,16]{0,2,1:T(8,128)(2,1)S(1)}, bf16[32,16,16]{0,2,1:T(8,128)(2,1)}, u32[]{:S(2)}) copy-start(bf16[32,16,16]{0,2,1:T(8,128)(2,1)} %param.10) | copy-start | bytes 49156
  39.3 48.6 %all-to-all-start.2 = ((bf16[16,2,32768]{2,1,0:T(2,128)(2,1)}), bf16[16,2,32768]{2,1,0:T(2,128)(2,1)S(1)}, u32[]{:S(2)}, u32[]{:S(2)}) async-start(bf16[16,2,32768]{2,1,0:T(2,128)(2,1)} %reshape.52), calls=%async_computation.2 | async-start | bytes 4194304 | tf_op jit(solution)/shard_map/all_to_all | solution.py:16
  46.8 353.7 %all-reduce.2.cloned.1.call-start = ((), (), s32[]{:S(2)}) async-start(), calls=%async_computation.4 | async-start | bytes 2097152 | tf_op jit(solution)/shard_map/psum | solution.py:34
  98.1 2.4 copy-start.2
  101.7 58.6 %copy-start.5 = (bf16[512,2048]{1,0:T(8,128)(2,1)S(1)}, bf16[512,2048]{1,0:T(8,128)(2,1)}, u32[]{:S(2)}) copy-start(bf16[512,2048]{1,0:T(8,128)(2,1)} %param.8) | copy-start | bytes 6291460
  101.8 58.6 %copy-start.6 = (bf16[512,2048]{1,0:T(8,128)(2,1)S(1)}, bf16[512,2048]{1,0:T(8,128)(2,1)}, u32[]{:S(2)}) copy-start(bf16[512,2048]{1,0:T(8,128)(2,1)} %param.7) | copy-start | bytes 6291460
  247.1 2.4 copy-start.4
  250.6 53.7 %copy-start.7 = (bf16[512,2048]{1,0:T(8,128)(2,1)S(1)}, bf16[512,2048]{1,0:T(8,128)(2,1)}, u32[]{:S(2)}) copy-start(bf16[512,2048]{1,0:T(8,128)(2,1)} %gather_fusion) | copy-start | bytes 6291460
  303.0 1.4 copy-start.8
  304.4 2.4 copy-start.3
  315.8 87.1 %copy-start.1 = (bf16[512,2048]{1,0:T(8,128)(2,1)S(1)}, bf16[512,2048]{1,0:T(8,128)(2,1)}, u32[]{:S(2)}) copy-start(bf16[512,2048]{1,0:T(8,128)(2,1)} %param.6) | copy-start | bytes 6291460
Sparse Core Ops, SparseCore 0:
  306.9 93.6 all-reduce.1
where the time goes:
time: 410 us
  blocking collectives  163 us (40%)
  waiting for transfers between devices  115 us (28%)
  local copies, waits for them, and re-layouts  57.6 us (14%)
  other arithmetic  33.1 us (8%)
  matrix products  18.5 us (5%)
  between operations  14.2 us (3%)
  starting transfers between devices  7.56 us (2%)
    psum x1, waiting for transfers between devices, per_device(): grad_block = lax.psum(partial_block, 'seq') / math.sqrt(count * width)  74.5 us
    all_to_all x1, blocking collectives, per_device(): lax.all_to_all(gated, 'seq', split_axis=0, concat_axis=1, tiled=True)  58.6 us
    all_to_all x1, blocking collectives, per_device(): lax.all_to_all(gate_grad[None], 'seq', split_axis=1, concat_axis=0, tiled...  52.4 us
    all_to_all x1, blocking collectives, per_device(): lax.all_to_all(back, 'seq', split_axis=0, concat_axis=1, tiled=True)  52.4 us
    all_to_all x1, waiting for transfers between devices, per_device(): lax.all_to_all(mixed[None], 'seq', split_axis=1, concat_axis=0, tiled=True)  40.9 us
    unnamed x31, local copies, waits for them, and re-layouts  28.9 us
    unnamed x2, other arithmetic  26.3 us
  transfers between devices with their start and end apart: 2, of which 2 were waited for; matrix products, arithmetic and copies ran while one was open for 5% of the time, Pallas kernels for 0%

commit v1 on v0

--- a/solution.py
+++ b/solution.py
@@ -31,7 +31,7 @@
     partial_block = lax.dot_general(
         back_rows, permuted, (((1,), (1,)), ((), ())), preferred_element_type=f32
     )
-    grad_block = lax.psum(partial_block, "seq") / math.sqrt(count * width)
+    grad_block = jnp.sum(lax.all_gather(partial_block, "seq"), axis=0) / math.sqrt(count * width)
     spread = lax.dot_general(
         block_factor, back_rows, (((0,), (0,)), ((), ())), preferred_element_type=f32
     ).astype(bf16)

time: 410 us -> 467 us (1.14); the launches traced: 410 us -> 459 us
  waiting for transfers between devices: 115 us -> 151 us
  blocking collectives: 163 us -> 172 us
  other arithmetic: 33.1 us -> 39.9 us
    all_gather x0 -> x1, waiting for transfers between devices: none -> 110 us  [per_device(): lax.all_gather(partial_block, 'seq')]
    psum x1 -> x0, waiting for transfers between devices: 74.5 us -> none  [per_device(): grad_block = lax.psum(partial_block, 'seq') / math.sqrt(count * width)]
    all_to_all x1, blocking collectives: 52.4 us -> 60.7 us  [per_device(): lax.all_to_all(back, 'seq', split_axis=0, concat_axis=1, tiled=True)]
    reduce_sum x0 -> x1, other arithmetic: none -> 8.05 us  [per_device(): jnp.sum(lax.all_gather(partial_block, 'seq'), axis=0)]
  transfers between devices with their start and end apart: 2 -> 2, of which waited for: 2 -> 2; matrix products, arithmetic and copies ran while one was open for 5% -> 4% of each run, Pallas kernels for 0% -> 0%
where the time goes in v1:
time: 467 us; the launch traced here: 459 us
  blocking collectives  172 us (37%)
  waiting for transfers between devices  151 us (32%)
  local copies, waits for them, and re-layouts  55.4 us (12%)
  other arithmetic  39.9 us (9%)
  matrix products  18.4 us (4%)
  between operations  14.2 us (3%)
  starting transfers between devices  7.56 us (2%)
    all_gather x1, waiting for transfers between devices, per_device(): lax.all_gather(partial_block, 'seq')  110 us
    all_to_all x1, blocking collectives, per_device(): lax.all_to_all(back, 'seq', split_axis=0, concat_axis=1, tiled=True)  60.7 us
    all_to_all x1, blocking collectives, per_device(): lax.all_to_all(gated, 'seq', split_axis=0, concat_axis=1, tiled=True)  58.9 us
    all_to_all x1, blocking collectives, per_device(): lax.all_to_all(gate_grad[None], 'seq', split_axis=1, concat_axis=0, tiled...  52.4 us
    all_to_all x1, waiting for transfers between devices, per_device(): lax.all_to_all(mixed[None], 'seq', split_axis=1, concat_axis=0, tiled=True)  40.9 us
    unnamed x31, local copies, waits for them, and re-layouts  28.8 us
    unnamed x2, other arithmetic  26.3 us
  transfers between devices with their start and end apart: 2, of which 2 were waited for; matrix products, arithmetic and copies ran while one was open for 4% of the time, Pallas kernels for 0%

profile of v1, /device:TPU:0, one launch (start us, length us, event | category | flops | bytes accessed | tf_op | source)
XLA Modules:
  0.0 458.8 jit_solution(8575304290987735815)
XLA Ops:
  7.2 0.0 copy-start
  7.2 0.8 compare_and_fusion
  8.0 0.7 compare_select_fusion
  8.7 0.1 copy-done
  8.8 3.3 gather_fusion
  12.1 0.0 copy-done.10
  12.1 3.1 fusion.3
  15.1 7.7 %copy.32 = bf16[1,512,2048]{2,0,1:T(2,128)(2,1)} copy(bf16[1,512,2048]{1,2,0:T(8,128)(2,1)S(1)} %fusion.3) | data formatting | bytes 4194304 | tf_op jit(solution)/shard_map/broadcast_in_dim | solution.py:16
  22.9 0.5 broadcast.9
  23.4 13.2 %reduce = bf16[512,2048]{1,0:T(8,128)(2,1)S(1)} reduce(bf16[512,1,2048]{2,1,0:T(2,128)(2,1)} %bitcast.33, bf16[]{:T(256)} %broadcast.9), dimensions={1}, to_apply=%bitcast.21.reduce_sub_computation | reduce | bytes 4194306
  36.5 2.8 reshape.53
  39.3 7.5 %all-to-all-start.2 = ((bf16[16,2,32768]{2,1,0:T(2,128)(2,1)}), bf16[16,2,32768]{2,1,0:T(2,128)(2,1)S(1)}, u32[]{:S(2)}, u32[]{:S(2)}) async-start(bf16[16,2,32768]{2,1,0:T(2,128)(2,1)} %reshape.53), calls=%async_computation.2 | async-start | bytes 4194304 | tf_op jit(solution)/shard_map/all_to_all | solution.py:16
  46.8 0.0 all-gather.3.cloned.1.call-start
  46.9 0.0 copy-done.9
  46.9 0.2 copy.34
  47.1 40.9 %all-to-all-done.2 = bf16[16,2,32768]{2,1,0:T(2,128)(2,1)S(1)} async-done(((bf16[16,2,32768]{2,1,0:T(2,128)(2,1)}), bf16[16,2,32768]{2,1,0:T(2,128)(2,1)S(1)}, u32[]{:S(2)}, u32[]{:S(2)}) %all-to-all-start.2) | async-done | bytes 2097184 | tf_op jit(solution)/shard_map/all_to_all | solution.py:16
  87.9 6.7 %reshape.54 = bf16[512,1,2048]{2,1,0:T(2,128)(2,1)} reshape(bf16[16,2,32768]{2,1,0:T(2,128)(2,1)S(1)} %all-to-all-done.2) | data formatting | bytes 4194304
  94.7 3.5 copy.40
  98.1 2.4 fusion.5
  100.6 0.0 copy-done.2
  100.6 1.2 copy.35
  101.7 0.0 copy-start.5
  101.8 0.0 copy-start.6
  101.8 58.9 %all_to_all.42 = bf16[16,32,2048]{2,1,0:T(8,128)(2,1)S(1)} all-to-all(bf16[16,32,2048]{2,1,0:T(8,128)(2,1)S(1)} %copy.35), channel_id=1, replica_groups=mesh['groups'=2,'seq'=16] {'seq'}, dimensions={0} | all-to-all | bytes 4194304 | tf_op jit(solution)/shard_map/all_to_all | solution.py:21
  160.7 0.0 copy-done.6
  160.7 3.0 fusion.1
  163.6 5.2 %copy.54 = bf16[1,512,2048]{2,0,1:T(2,128)(2,1)} copy(bf16[1,512,2048]{2,1,0:T(8,128)(2,1)S(1)} %get-tuple-element.17) | data formatting | bytes 4194304 | tf_op jit(solution)/shard_map/broadcast_in_dim | solution.py:17
  168.8 13.2 %reduce.1 = bf16[512,2048]{1,0:T(8,128)(2,1)S(1)} reduce(bf16[512,1,2048]{2,1,0:T(2,128)(2,1)} %bitcast.34, bf16[]{:T(256)} %broadcast.9), dimensions={1}, to_apply=%bitcast.30.reduce_sub_computation | reduce | bytes 4194306
  182.0 2.8 reshape.51
  184.8 52.4 %all_to_all.43 = bf16[16,2,32768]{2,1,0:T(2,128)(2,1)S(1)} all-to-all(bf16[16,2,32768]{2,1,0:T(2,128)(2,1)} %reshape.51), channel_id=1, replica_groups=mesh['groups'=2,'seq'=16] {'seq'}, dimensions={0} | all-to-all | bytes 4194304 | tf_op jit(solution)/shard_map/all_to_all | solution.py:17
  237.2 6.7 %reshape.52 = bf16[512,1,2048]{2,1,0:T(2,128)(2,1)} reshape(bf16[16,2,32768]{2,1,0:T(2,128)(2,1)S(1)} %all_to_all.43) | data formatting | bytes 4194304
  243.9 3.5 copy.39
  247.4 2.4 fusion.4
  249.8 1.2 copy.30
  250.9 0.0 copy-start.7
  251.0 60.7 %all_to_all.44 = bf16[16,32,2048]{2,1,0:T(8,128)(2,1)S(1)} all-to-all(bf16[16,32,2048]{2,1,0:T(8,128)(2,1)S(1)} %copy.30), channel_id=1, replica_groups=mesh['groups'=2,'seq'=16] {'seq'}, dimensions={0} | all-to-all | bytes 4194304 | tf_op jit(solution)/shard_map/all_to_all | solution.py:28
  311.7 1.3 copy-done.8
  313.0 2.3 fusion.19
  315.3 0.0 all-gather.3.cloned.1.call-update
  315.3 0.0 copy-done.3
  315.3 3.9 fusion.12
  319.2 0.8 copy.38
  320.1 4.2 fusion.2
  324.3 3.0 copy.31
  327.3 5.1 %scatter_custom_fusion = bf16[512,2048]{1,0:T(8,128)(2,1)} fusion(s32[512]{0:T(512)S(1)} %compare_select_fusion, bf16[512,2048]{1,0:T(8,128)(2,1)S(1)} %copy.31, bf16[]{:T(256)} %constant.8.clone.1), kind=kCustom, calls=%fused_computation.22 | custom fusion | bytes 2097154 | tf_op jit(solution)/shard_map/scatter | solution.py:38
  332.4 110.4 %all-gather.3.cloned.1.call-done = f32[8192,512]{1,0:T(8,128)} async-done(((f32[512,512]{1,0:T(8,128)}), f32[8192,512]{1,0:T(8,128)}) %all-gather.3.cloned.1.call-update) | async-done | bytes 16777232 | tf_op jit(solution)/shard_map/all_gather | solution.py:34
  442.8 8.1 %reduce_sum.9 = f32[512,512]{1,0:T(8,128)S(1)} reduce(f32[16,512,512]{2,1,0:T(8,128)} %bitcast.32, f32[]{:T(128)} %constant.25.clone.1), dimensions={0}, to_apply=%region_1.2 | reduce | flops 3932160 | bytes 17825796 | tf_op jit(solution)/shard_map/reduce_sum | solution.py:34
  450.8 1.1 broadcast_multiply_fusion
  (12 shorter events, 0.0 us)
Async XLA Ops:
  7.2 1.6 copy-start
  8.8 3.3 copy-start.10
  39.3 7.6 %copy-start.9 = (bf16[32,16,16]{0,2,1:T(8,128)(2,1)S(1)}, bf16[32,16,16]{0,2,1:T(8,128)(2,1)}, u32[]{:S(2)}) copy-start(bf16[32,16,16]{0,2,1:T(8,128)(2,1)} %param.10) | copy-start | bytes 49156
  39.3 48.6 %all-to-all-start.2 = ((bf16[16,2,32768]{2,1,0:T(2,128)(2,1)}), bf16[16,2,32768]{2,1,0:T(2,128)(2,1)S(1)}, u32[]{:S(2)}, u32[]{:S(2)}) async-start(bf16[16,2,32768]{2,1,0:T(2,128)(2,1)} %reshape.53), calls=%async_computation.2 | async-start | bytes 4194304 | tf_op jit(solution)/shard_map/all_to_all | solution.py:16
  46.8 396.0 %all-gather.3.cloned.1.call-start = ((), (), s32[]{:S(2)}) async-start(), calls=%async_computation.4 | async-start | bytes 17825792 | tf_op jit(solution)/shard_map/all_gather | solution.py:34
  98.1 2.4 copy-start.2
  101.7 58.9 %copy-start.5 = (bf16[512,2048]{1,0:T(8,128)(2,1)S(1)}, bf16[512,2048]{1,0:T(8,128)(2,1)}, u32[]{:S(2)}) copy-start(bf16[512,2048]{1,0:T(8,128)(2,1)} %param.8) | copy-start | bytes 6291460
  101.8 58.9 %copy-start.6 = (bf16[512,2048]{1,0:T(8,128)(2,1)S(1)}, bf16[512,2048]{1,0:T(8,128)(2,1)}, u32[]{:S(2)}) copy-start(bf16[512,2048]{1,0:T(8,128)(2,1)} %param.7) | copy-start | bytes 6291460
  247.4 2.4 copy-start.4
  250.9 62.0 %copy-start.7 = (bf16[512,2048]{1,0:T(8,128)(2,1)S(1)}, bf16[512,2048]{1,0:T(8,128)(2,1)}, u32[]{:S(2)}) copy-start(bf16[512,2048]{1,0:T(8,128)(2,1)} %gather_fusion) | copy-start | bytes 6291460
  311.7 1.3 copy-start.8
  313.0 2.4 copy-start.3
  442.8 9.1 %copy-start.1 = (bf16[512,2048]{1,0:T(8,128)(2,1)S(1)}, bf16[512,2048]{1,0:T(8,128)(2,1)}, u32[]{:S(2)}) copy-start(bf16[512,2048]{1,0:T(8,128)(2,1)} %param.6) | copy-start | bytes 6291460
Sparse Core Ops, SparseCore 0:
  315.5 127.2 all-gather.2
